TPU v7x, 32 devices: a whole 2x2x4 slice. The times are simulated.
32 devices in a mesh: orb: 4 (over z), tile: 8 (over y, x, core).
Axes of the slice: x: 2, y: 2, z: 4, core: 2. Of those that a mesh axis runs over, the one named last changes fastest.
Arguments:
- basis_values: bfloat16 [2048, 65536], P('tile'), may hold values from -6 to 6
- coefficients: bfloat16 [65536, 128], P('tile', 'orb'), may hold values from -0.03125 to 0.03125
- occupations: float32 [128], P('orb'), may hold values from 0.5 to 2
- owners: int32 [2048, 1], P('tile'), may hold values from 0 to 7; in each aligned block of 256 rows (0 to 255, 256 to 511, ...) at most 64 rows name the same one
- offsets: int32 [2048], P('tile'), may hold values from 0 to 8191
Outputs:
- density: float32 [64, 64, 128], P('tile', 'orb')
- gradient: float32 [3, 64, 64, 128], P(None, 'tile', 'orb')
Inputs may be any that keep to these rules, and one draw needn't show every extreme that they name: `owners`: at most 64 entries of one tile's list name the same owner, and some tile's list reaches 64.
All inputs are finite; a program needn't handle non-finite values.
Results may differ from a plain program's by a relative error of at most 0.0003.
Values may be sent and summed in bfloat16 or wider, within the bound.
A program may use at most 320 MiB of HBM per device.

v0:
```python
import jax
import jax.numpy as jnp
from jax import lax
from jax.sharding import PartitionSpec as P

CY = 64
CZ = 128


def with_halo(cells, sides, width):
    for axis, dim in sides:
        count = lax.axis_size(axis)
        ends = count - 1
        head = lax.slice_in_dim(cells, 0, width, axis=dim)
        tail = lax.slice_in_dim(cells, cells.shape[dim] - width, cells.shape[dim], axis=dim)
        cells = jnp.concatenate(
            [
                lax.ppermute(tail, axis, [(i, (i + 1) % count) for i in range(ends)]),
                cells,
                lax.ppermute(head, axis, [((i + 1) % count, i) for i in range(ends)]),
            ],
            axis=dim,
        )
    return cells


def central(padded):
    along_x = 0.5 * (padded[2:, 1:-1, 1:-1] - padded[:-2, 1:-1, 1:-1])
    along_y = 0.5 * (padded[1:-1, 2:, 1:-1] - padded[1:-1, :-2, 1:-1])
    along_z = 0.5 * (padded[1:-1, 1:-1, 2:] - padded[1:-1, 1:-1, :-2])
    return jnp.stack([along_x, along_y, along_z])


def body(basis_values, coefficients, occupations, owners, offsets):
    listed_count = owners.shape[0]
    rows_held = coefficients.shape[0]
    local_orbitals = coefficients.shape[1]
    owner_ids = owners[:, 0]
    global_rows = owner_ids * rows_held + offsets
    empty = jnp.zeros((listed_count, local_orbitals), jnp.bfloat16)
    shard_rows = lax.all_gather(coefficients, "tile", axis=0, tiled=True)
    inside = (global_rows >= 0) & (global_rows < shard_rows.shape[0])
    safe_rows = jnp.clip(global_rows, 0, shard_rows.shape[0] - 1)
    taken = jnp.take(shard_rows, safe_rows, axis=0)
    listed = jnp.where(inside[:, None], taken, empty)
    depth_cells = basis_values.shape[1] // (CY * CZ)
    share_width = CY // lax.axis_size("orb")
    orbitals = jnp.einsum("bo,bc->oc", listed, basis_values, preferred_element_type=jnp.float32)
    partial_value = jnp.sum(occupations[:, None] * orbitals * orbitals, axis=0).reshape(
        depth_cells, CY, CZ
    )
    density_full = lax.psum(partial_value, "orb")
    padded = with_halo(density_full, (("tile", 0),), 1)
    padded = jnp.pad(padded, ((0, 0), (1, 1), (1, 1)))
    first_col = lax.axis_index("orb") * share_width
    density = lax.dynamic_slice_in_dim(density_full, first_col, share_width, 1)
    gradient = lax.dynamic_slice_in_dim(central(padded), first_col, share_width, 2)
    return (density, gradient)


def solution(mesh):
    placed = (P("tile", None), P("tile", "orb"), P("orb"), P("tile", None), P("tile"))
    return jax.shard_map(
        body,
        mesh=mesh,
        in_specs=placed,
        out_specs=(P("tile", "orb", None), P(None, "tile", "orb", None)),
        check_vma=False,
    )
```

profile of v0, /device:TPU:4, one launch (start us, length us, event | category | flops | bytes accessed | tf_op | source)
XLA Modules:
  0.0 181.8 jit_solution(3366293693858491619)
XLA Ops:
  7.2 0.0 all-gather.2.cloned.1.call-start
  7.2 2.7 %copy.7 = bf16[8192,32]{1,0:T(8,128)(2,1)} copy(bf16[8192,32]{0,1:T(8,128)(2,1)} %param.6) | data formatting | bytes 1048576 | tf_op args[1]
  9.9 0.0 all-gather.2.cloned.1.call-update
  9.9 0.0 all-reduce.3.cloned.1.call-start
  10.0 0.7 broadcast_multiply_fusion
  10.6 0.7 compare_and_fusion
  11.3 88.9 %all-gather.2.cloned.1.call-done = bf16[65536,32]{1,0:T(8,128)(2,1)} async-done(((bf16[8192,32]{1,0:T(8,128)(2,1)}), bf16[65536,32]{1,0:T(8,128)(2,1)}) %all-gather.2.cloned.1.call-update) | async-done | bytes 4194320 | tf_op jit(solution)/shard_map/all_gather | solution.py:41
  100.3 8.7 %gather_fusion = bf16[256,32]{1,0:T(8,128)(2,1)S(1)} fusion(bf16[65536,32]{1,0:T(8,128)(2,1)} %all-gather.2.cloned.1.call-done, s32[1024]{0:T(1024)S(1)} %pad_clamp_fusion), kind=kCustom, calls=%fused_computation | custom fusion | bytes 33792 | tf_op jit(solution)/shard_map/jit(_take)/gather | solution.py:44
  108.9 17.4 %fusion = f32[65536]{0:T(1024)} fusion(f32[32]{0:T(128)} %param.7, bf16[256,65536]{1,0:T(8,128)(2,1)} %param.5, bf16[256,32]{1,0:T(8,128)(2,1)S(1)} %gather_fusion, pred[256]{0:T(512)(128)(4,1)S(1)} %get-tuple-element.2, pred[256]{0:T(512)(128)(4,1)S(1)} %get-tuple-element.8), kind=kOutput, calls=%fused_computation.2 | convolution fusion | flops 1079984128 | bytes 33833600 | tf_op jit(solution)/shard_map/bo,bc->oc/dot_general | solution.py:48
  126.3 0.0 all-reduce.3.cloned.1.call-update
  126.4 36.5 %all-reduce.3.cloned.1.call-done = f32[8,64,128]{2,1,0:T(8,128)} async-done(((f32[8,64,128]{2,1,0:T(8,128)}), f32[8,64,128]{2,1,0:T(8,128)}) %all-reduce.3.cloned.1.call-update) | async-done | bytes 262160 | tf_op jit(solution)/shard_map/psum | solution.py:52
  162.8 0.8 fusion.24
  163.6 1.9 %collective-permute-start = (f32[1,64,128]{2,1,0:T(8,128)S(1)}, f32[1,64,128]{2,1,0:T(8,128)S(1)}, u32[]{:S(2)}, u32[]{:S(2)}) collective-permute-start(f32[1,64,128]{2,1,0:T(8,128)S(1)} %get-tuple-element.6), channel_id=1, source_target_pairs={{1,0},{2,1},{3,2},{4,3},{5,4},{6,5},{7,6},{9,8},{10,9},{11,10},{12... | collective-permute-start | bytes 98312 | tf_op jit(solution)/shard_map/ppermute | solution.py:20
  165.5 2.4 %collective-permute-start.1 = (f32[1,64,128]{2,1,0:T(8,128)S(1)}, f32[1,64,128]{2,1,0:T(8,128)S(1)}, u32[]{:S(2)}, u32[]{:S(2)}) collective-permute-start(f32[1,64,128]{2,1,0:T(8,128)S(1)} %get-tuple-element.7), channel_id=1, source_target_pairs={{0,1},{1,2},{2,3},{3,4},{4,5},{5,6},{6,7},{8,9},{9,10},{10,11},{11... | collective-permute-start | bytes 98312 | tf_op jit(solution)/shard_map/ppermute | solution.py:18
  167.9 1.5 constant_dynamic-slice_fusion
  169.4 0.0 collective-permute-done
  169.4 2.2 %collective-permute-done.1 = f32[1,64,128]{2,1,0:T(8,128)S(1)} collective-permute-done((f32[1,64,128]{2,1,0:T(8,128)S(1)}, f32[1,64,128]{2,1,0:T(8,128)S(1)}, u32[]{:S(2)}, u32[]{:S(2)}) %collective-permute-start.1) | collective-permute-done | bytes 32800 | tf_op jit(solution)/shard_map/ppermute | solution.py:18
  171.7 1.2 select_maximum_fusion
  172.9 1.3 fusion.5
  174.2 0.7 fusion.12
  (1 shorter events, 0.0 us)
Async XLA Ops:
  7.2 93.1 %all-gather.2.cloned.1.call-start = ((), (), s32[]{:S(2)}) async-start(), calls=%async_computation | async-start | bytes 18874368 | tf_op jit(solution)/shard_map/all_gather | solution.py:41
  9.9 152.9 %all-reduce.3.cloned.1.call-start = ((), (), s32[]{:S(2)}) async-start(), calls=%async_computation.1 | async-start | bytes 524288 | tf_op jit(solution)/shard_map/psum | solution.py:52
  163.6 5.8 %collective-permute-start = (f32[1,64,128]{2,1,0:T(8,128)S(1)}, f32[1,64,128]{2,1,0:T(8,128)S(1)}, u32[]{:S(2)}, u32[]{:S(2)}) collective-permute-start(f32[1,64,128]{2,1,0:T(8,128)S(1)} %get-tuple-element.6), channel_id=1, source_target_pairs={{1,0},{2,1},{3,2},{4,3},{5,4},{6,5},{7,6},{9,8},{10,9},{11,10},{12... | collective-permute-start | bytes 98312 | tf_op jit(solution)/shard_map/ppermute | solution.py:20
  165.5 6.1 %collective-permute-start.1 = (f32[1,64,128]{2,1,0:T(8,128)S(1)}, f32[1,64,128]{2,1,0:T(8,128)S(1)}, u32[]{:S(2)}, u32[]{:S(2)}) collective-permute-start(f32[1,64,128]{2,1,0:T(8,128)S(1)} %get-tuple-element.7), channel_id=1, source_target_pairs={{0,1},{1,2},{2,3},{3,4},{4,5},{5,6},{6,7},{8,9},{9,10},{10,11},{11... | collective-permute-start | bytes 98312 | tf_op jit(solution)/shard_map/ppermute | solution.py:18
Sparse Core Ops, SparseCore 0:
  10.0 90.1 all-gather.1
  126.5 36.3 all-reduce.2
where the time goes:
time: 182 us
  waiting for transfers between devices  128 us (70%)
  matrix products  17.4 us (10%)
  between operations  14.1 us (8%)
  local copies, waits for them, and re-layouts  13.6 us (7%)
  other arithmetic  4.62 us (3%)
  starting transfers between devices  4.39 us (2%)
    all_gather x1, waiting for transfers between devices, body(): shard_rows = lax.all_gather(coefficients, 'tile', axis=0, tiled=True)  88.9 us
    psum x1, waiting for transfers between devices, body(): density_full = lax.psum(partial_value, 'orb')  36.5 us
    dot_general x1, matrix products, body(): jnp.einsum('bo,bc->oc', listed, basis_values, preferred_element_type=jnp....  17.4 us
    gather x1, local copies, waits for them, and re-layouts, body(): taken = jnp.take(shard_rows, safe_rows, axis=0)  8.65 us
  transfers between devices with their start and end apart: 4, of which 3 were waited for; matrix products, arithmetic and copies ran while one was open for 2% of the time, Pallas kernels for 0%

commit v1 on v0

--- a/solution.py
+++ b/solution.py
@@ -49,7 +49,7 @@
     partial_value = jnp.sum(occupations[:, None] * orbitals * orbitals, axis=0).reshape(
         depth_cells, CY, CZ
     )
-    density_full = lax.psum(partial_value, "orb")
+    density_full = jnp.sum(lax.all_gather(partial_value, "orb"), axis=0)
     padded = with_halo(density_full, (("tile", 0),), 1)
     padded = jnp.pad(padded, ((0, 0), (1, 1), (1, 1)))
     first_col = lax.axis_index("orb") * share_width

time: 182 us -> 173 us (0.951)
  waiting for transfers between devices: 128 us -> 121 us
    psum x1 -> x0, waiting for transfers between devices: 36.5 us -> none  [body(): density_full = lax.psum(partial_value, 'orb')]
    all_gather x0 -> x1, waiting for transfers between devices: none -> 28.9 us  [body(): density_full = jnp.sum(lax.all_gather(partial_value, 'orb'), axis=0)]
  transfers between devices with their start and end apart: 4 -> 4, of which waited for: 3 -> 3; matrix products, arithmetic and copies ran while one was open for 2% -> 1% of each run, Pallas kernels for 0% -> 0%
where the time goes in v1:
time: 173 us
  waiting for transfers between devices  121 us (70%)
  matrix products  17.4 us (10%)
  between operations  14.1 us (8%)
  local copies, waits for them, and re-layouts  12 us (7%)
  starting transfers between devices  4.41 us (3%)
  other arithmetic  3.92 us (2%)
    all_gather x1, waiting for transfers between devices, body(): shard_rows = lax.all_gather(coefficients, 'tile', axis=0, tiled=True)  88.9 us
    all_gather x1, waiting for transfers between devices, body(): density_full = jnp.sum(lax.all_gather(partial_value, 'orb'), axis=0)  28.9 us
    dot_general x1, matrix products, body(): jnp.einsum('bo,bc->oc', listed, basis_values, preferred_element_type=jnp....  17.4 us
    gather x1, local copies, waits for them, and re-layouts, body(): taken = jnp.take(shard_rows, safe_rows, axis=0)  8.65 us
    ppermute x1, waiting for transfers between devices, with_halo(): lax.ppermute(tail, axis, [(i, (i + 1) % count) for i in range(ends)])  3.48 us
  transfers between devices with their start and end apart: 4, of which 3 were waited for; matrix products, arithmetic and copies ran while one was open for 1% of the time, Pallas kernels for 0%

profile of v1, /device:TPU:4, one launch (start us, length us, event | category | flops | bytes accessed | tf_op | source)
XLA Modules:
  0.0 173.1 jit_solution(10452355087205392284)
XLA Ops:
  7.2 0.0 all-gather.3.cloned.1.call-start
  7.2 2.7 %copy.8 = bf16[8192,32]{1,0:T(8,128)(2,1)} copy(bf16[8192,32]{0,1:T(8,128)(2,1)} %param.6) | data formatting | bytes 1048576 | tf_op args[1]
  9.9 0.0 all-gather.3.cloned.1.call-update
  9.9 0.0 all-gather.5.cloned.1.call-start
  10.0 0.7 broadcast_multiply_fusion
  10.6 0.7 compare_and_fusion
  11.3 88.9 %all-gather.3.cloned.1.call-done = bf16[65536,32]{1,0:T(8,128)(2,1)} async-done(((bf16[8192,32]{1,0:T(8,128)(2,1)}), bf16[65536,32]{1,0:T(8,128)(2,1)}) %all-gather.3.cloned.1.call-update) | async-done | bytes 4194320 | tf_op jit(solution)/shard_map/all_gather | solution.py:41
  100.3 8.7 %gather_fusion = bf16[256,32]{1,0:T(8,128)(2,1)S(1)} fusion(bf16[65536,32]{1,0:T(8,128)(2,1)} %all-gather.3.cloned.1.call-done, s32[1024]{0:T(1024)S(1)} %pad_clamp_fusion), kind=kCustom, calls=%fused_computation | custom fusion | bytes 33792 | tf_op jit(solution)/shard_map/jit(_take)/gather | solution.py:44
  108.9 17.4 %fusion = f32[65536]{0:T(1024)} fusion(f32[32]{0:T(128)} %param.7, bf16[256,65536]{1,0:T(8,128)(2,1)} %param.5, bf16[256,32]{1,0:T(8,128)(2,1)S(1)} %gather_fusion, pred[256]{0:T(512)(128)(4,1)S(1)} %get-tuple-element.2, pred[256]{0:T(512)(128)(4,1)S(1)} %get-tuple-element.8), kind=kOutput, calls=%fused_computation.2 | convolution fusion | flops 1079984128 | bytes 33833600 | tf_op jit(solution)/shard_map/bo,bc->oc/dot_general | solution.py:48
  126.3 0.0 all-gather.5.cloned.1.call-update
  126.4 28.9 %all-gather.5.cloned.1.call-done = f32[4,8,64,128]{3,2,1,0:T(8,128)} async-done(((f32[1,8,64,128]{3,2,1,0:T(8,128)}), f32[4,8,64,128]{3,2,1,0:T(8,128)}) %all-gather.5.cloned.1.call-update) | async-done | bytes 1048592 | tf_op jit(solution)/shard_map/all_gather | solution.py:52
  155.2 1.3 reduce_sum.19
  156.5 2.3 %collective-permute-start = (f32[1,64,128]{2,1,0:T(8,128)S(1)}, f32[1,64,128]{2,1,0:T(8,128)S(1)}, u32[]{:S(2)}, u32[]{:S(2)}) collective-permute-start(f32[1,64,128]{2,1,0:T(8,128)S(1)} %get-tuple-element.6), channel_id=1, source_target_pairs={{1,0},{2,1},{3,2},{4,3},{5,4},{6,5},{7,6},{9,8},{10,9},{11,10},{12... | collective-permute-start | bytes 98312 | tf_op jit(solution)/shard_map/ppermute | solution.py:20
  158.9 2.0 %collective-permute-start.1 = (f32[1,64,128]{2,1,0:T(8,128)S(1)}, f32[1,64,128]{2,1,0:T(8,128)S(1)}, u32[]{:S(2)}, u32[]{:S(2)}) collective-permute-start(f32[1,64,128]{2,1,0:T(8,128)S(1)} %get-tuple-element.7), channel_id=1, source_target_pairs={{0,1},{1,2},{2,3},{3,4},{4,5},{5,6},{6,7},{8,9},{9,10},{10,11},{11... | collective-permute-start | bytes 98312 | tf_op jit(solution)/shard_map/ppermute | solution.py:18
  160.9 0.6 constant_dynamic-slice_fusion
  161.5 0.0 collective-permute-done
  161.5 3.5 %collective-permute-done.1 = f32[1,64,128]{2,1,0:T(8,128)S(1)} collective-permute-done((f32[1,64,128]{2,1,0:T(8,128)S(1)}, f32[1,64,128]{2,1,0:T(8,128)S(1)}, u32[]{:S(2)}, u32[]{:S(2)}) %collective-permute-start.1) | collective-permute-done | bytes 32800 | tf_op jit(solution)/shard_map/ppermute | solution.py:18
  165.0 0.3 select_maximum_fusion
  165.3 0.3 fusion.5
  165.6 0.7 fusion.12
  (2 shorter events, 0.0 us)
Async XLA Ops:
  7.2 93.1 %all-gather.3.cloned.1.call-start = ((), (), s32[]{:S(2)}) async-start(), calls=%async_computation | async-start | bytes 18874368 | tf_op jit(solution)/shard_map/all_gather | solution.py:41
  9.9 145.3 %all-gather.5.cloned.1.call-start = ((), (), s32[]{:S(2)}) async-start(), calls=%async_computation.1 | async-start | bytes 1310720 | tf_op jit(solution)/shard_map/all_gather | solution.py:52
  156.5 5.0 %collective-permute-start = (f32[1,64,128]{2,1,0:T(8,128)S(1)}, f32[1,64,128]{2,1,0:T(8,128)S(1)}, u32[]{:S(2)}, u32[]{:S(2)}) collective-permute-start(f32[1,64,128]{2,1,0:T(8,128)S(1)} %get-tuple-element.6), channel_id=1, source_target_pairs={{1,0},{2,1},{3,2},{4,3},{5,4},{6,5},{7,6},{9,8},{10,9},{11,10},{12... | collective-permute-start | bytes 98312 | tf_op jit(solution)/shard_map/ppermute | solution.py:20
  158.9 6.1 %collective-permute-start.1 = (f32[1,64,128]{2,1,0:T(8,128)S(1)}, f32[1,64,128]{2,1,0:T(8,128)S(1)}, u32[]{:S(2)}, u32[]{:S(2)}) collective-permute-start(f32[1,64,128]{2,1,0:T(8,128)S(1)} %get-tuple-element.7), channel_id=1, source_target_pairs={{0,1},{1,2},{2,3},{3,4},{4,5},{5,6},{6,7},{8,9},{9,10},{10,11},{11... | collective-permute-start | bytes 98312 | tf_op jit(solution)/shard_map/ppermute | solution.py:18
Sparse Core Ops, SparseCore 0:
  10.0 90.1 all-gather.2
  126.5 28.7 all-gather.4
